TPU v7x, 512 devices: a whole 4x8x8 slice. The times are simulated.
512 devices in a mesh: dp: 64 (over z, x, core), expert: 8 (over y).
Axes of the slice: x: 4, y: 8, z: 8, core: 2. Of those that a mesh axis runs over, the one named last changes fastest.
Arguments:
- tokens: bfloat16 [512, 4096], P('expert', 'dp'), may hold values from -6 to 6
- cotangent: bfloat16 [512, 4096], P('expert', 'dp'), may hold values from -6 to 6
- gate_logit: float32 [512], P('expert'), may hold values from -8 to 8
- routes: int32 [512, 2], P('expert'), may hold values from 0 to 7, all different within a row; in each aligned block of 64 rows (0 to 63, 64 to 127, ...) at most 32 rows name the same one
- w_up: bfloat16 [8, 14336, 4096], P('expert', 'dp'), may hold values from -0.09375 to 0.09375
- w_down: bfloat16 [8, 14336, 4096], P('expert', 'dp'), may hold values from -0.046875 to 0.046875
- basis: bfloat16 [4096, 256], P('dp'), may hold values from -0.09375 to 0.09375
- sketch: float32 [8, 256, 256], P('expert'), may hold values from -1 to 10, as said below
Outputs:
- token_grad: bfloat16 [512, 4096], P('expert', 'dp')
- sketch_next: float32 [8, 256, 256], P('expert')
- precond: float32 [8, 14336, 256], P('expert', 'dp')
Inputs may be any that keep to these rules, and one draw needn't show every extreme that they name: `routes`: each row names 2 different experts. Among the 64 tokens of one index of expert at most 32 name the same expert, and in some index that many do. `sketch`: each matrix is symmetric, and in every row its diagonal entry exceeds the sum of the magnitudes off the diagonal.
All inputs are finite; a program needn't handle non-finite values.
Results may differ from a plain program's by a relative error of at most 0.0064.
Values may be sent and summed in bfloat16 or wider, within the bound.
A program may use at most 128 MiB of HBM per device.

v0:
```python
import jax
import jax.numpy as jnp
from jax import lax
from jax.sharding import PartitionSpec as P

decay_rate = 0.9
damping = 1.0
highest = lax.Precision.HIGHEST


def per_device(tokens, cotangent, gate_logit, routes, w_up, w_down, basis, sketch):
    experts = lax.axis_size("expert")
    tok_rows = tokens.shape[0]
    width_local = tokens.shape[1]
    capacity = min(tok_rows, tok_rows * 4 // experts)
    slot_count = experts * capacity
    gate_first = jax.nn.sigmoid(gate_logit)
    gates = jnp.stack([gate_first, 1.0 - gate_first], axis=1)
    expert_ids = jnp.arange(experts, dtype=jnp.int32)
    chosen = routes[:, :, None] == expert_ids[None, None, :]
    hit_count = jnp.sum(chosen.astype(jnp.int32), axis=1)
    gate_by_expert = jnp.sum(chosen.astype(jnp.float32) * gates[:, :, None], axis=1)
    before = jnp.cumsum(hit_count, axis=0) - hit_count
    slot_of = expert_ids[None, :] * capacity + before
    slot_ids = jnp.arange(slot_count, dtype=jnp.int32)
    slot_match = (
        (slot_of[None, :, :] == slot_ids[:, None, None]) & (hit_count[None, :, :] > 0)
    ).astype(jnp.float32)
    table = jnp.sum(slot_match, axis=2)
    gate_slot = jnp.sum(slot_match * gate_by_expert[None, :, :], axis=(1, 2))
    table_b = table.astype(jnp.bfloat16)
    x_send = jnp.dot(table_b, tokens, preferred_element_type=jnp.float32).astype(jnp.bfloat16)
    cot_rows = jnp.dot(table_b, cotangent, preferred_element_type=jnp.float32)
    dy_send = (gate_slot[:, None] * cot_rows).astype(jnp.bfloat16)
    x_send = x_send.reshape(experts, capacity, width_local)
    dy_send = dy_send.reshape(experts, capacity, width_local)
    x_recv, dy_recv = (
        lax.all_to_all(x_send, "expert", split_axis=0, concat_axis=0, tiled=True),
        lax.all_to_all(dy_send, "expert", split_axis=0, concat_axis=0, tiled=True),
    )
    x_full, dy_full = (
        lax.all_gather(x_recv, "dp", axis=2, tiled=True),
        lax.all_gather(dy_recv, "dp", axis=2, tiled=True),
    )
    row_block = x_full.reshape(slot_count, -1)
    dy_block = dy_full.reshape(slot_count, -1)
    up_local = w_up[0]
    down_local = w_down[0]
    hidden = lax.dot_general(
        row_block, up_local, (((1,), (1,)), ((), ())), preferred_element_type=jnp.float32
    )
    back_grad = lax.dot_general(
        dy_block, down_local, (((1,), (1,)), ((), ())), preferred_element_type=jnp.float32
    )
    sigma_val = jax.nn.sigmoid(hidden)
    hidden_grad = (back_grad * sigma_val * (1.0 + hidden * (1.0 - sigma_val))).astype(jnp.bfloat16)
    partial_value = jnp.dot(hidden_grad, up_local, preferred_element_type=jnp.float32)
    summed = lax.psum_scatter(partial_value, "dp", scatter_dimension=1, tiled=True).astype(
        jnp.bfloat16
    )
    returned = lax.all_to_all(
        summed.reshape(experts, capacity, width_local),
        "expert",
        split_axis=0,
        concat_axis=0,
        tiled=True,
    )
    token_grad = lax.dot_general(
        table_b,
        returned.reshape(slot_count, width_local),
        (((0,), (0,)), ((), ())),
        preferred_element_type=jnp.float32,
    ).astype(jnp.bfloat16)
    basis_full = lax.all_gather(basis, "dp", axis=0, tiled=True)
    projected = jnp.dot(row_block, basis_full, preferred_element_type=jnp.float32).astype(
        jnp.bfloat16
    )
    coefficients = lax.dot_general(
        projected, hidden_grad, (((0,), (0,)), ((), ())), preferred_element_type=jnp.float32
    )
    gram_part = jnp.dot(coefficients, coefficients.T, precision=highest)
    total_hidden = w_up.shape[1] * lax.axis_size("dp")
    gram_total = lax.psum(gram_part, "dp") / total_hidden
    merged = decay_rate * sketch[0] + gram_total
    factor = jnp.linalg.cholesky(merged + damping * jnp.eye(merged.shape[0], dtype=jnp.float32))
    solved = damping * jax.scipy.linalg.cho_solve((factor, True), coefficients)
    return (token_grad, merged[None], solved.T[None])


def solution(mesh):
    in_specs = (
        P("expert", "dp"),
        P("expert", "dp"),
        P("expert"),
        P("expert", None),
        P("expert", "dp", None),
        P("expert", "dp", None),
        P("dp", None),
        P("expert", None, None),
    )
    out_specs = (P("expert", "dp"), P("expert", None, None), P("expert", "dp", None))
    return jax.shard_map(
        per_device, mesh=mesh, in_specs=in_specs, out_specs=out_specs, check_vma=False
    )
```

profile of v0, /device:TPU:2, one launch (start us, length us, event | category | flops | bytes accessed | tf_op | source)
XLA Modules:
  0.0 657.5 jit_solution(2081533431602891325)
XLA Ops:
  7.2 0.8 convert_reduce_fusion.1
  10.1 0.9 fusion.16
  11.3 14.9 %all_to_all.15 = bf16[8,2,1024]{2,1,0:T(2,128)(2,1)S(1)} all-to-all(bf16[8,2,1024]{2,1,0:T(2,128)(2,1)S(1)} %reshape.113), channel_id=1, replica_groups=mesh['dp'=64,'expert'=8] {'expert'}, dimensions={0} | all-to-all | bytes 65536 | tf_op jit(solution)/shard_map/all_to_all | solution.py:39
  26.3 0.8 copy.44
  27.2 0.9 convolution_convert_fusion.1
  28.3 10.4 %all_to_all.16 = bf16[8,2,1024]{2,1,0:T(2,128)(2,1)S(1)} all-to-all(bf16[8,2,1024]{2,1,0:T(2,128)(2,1)S(1)} %reshape.115), channel_id=1, replica_groups=mesh['dp'=64,'expert'=8] {'expert'}, dimensions={0} | all-to-all | bytes 65536 | tf_op jit(solution)/shard_map/all_to_all | solution.py:38
  38.9 0.8 copy.47
  40.5 74.2 %all-gather.4.cloned.1.call-done = bf16[8,32,4096]{1,0,2:T(8,128)(2,1)} async-done(((bf16[8,32,64]{1,0,2:T(8,128)(2,1)}), bf16[8,32,4096]{1,0,2:T(8,128)(2,1)}) %all-gather.4.cloned.1.call-update) | async-done | bytes 2097168 | tf_op jit(solution)/shard_map/all_gather | solution.py:43
  114.7 9.3 %copy.45 = bf16[8,32,4096]{2,1,0:T(8,128)(2,1)} copy(bf16[8,32,4096]{1,0,2:T(8,128)(2,1)} %all-gather.4.cloned.1.call-done) | data formatting | bytes 4194304 | tf_op jit(solution)/shard_map/all_gather | solution.py:43
  124.0 80.1 %all-gather.6.cloned.1.call-done = bf16[8,32,4096]{1,0,2:T(8,128)(2,1)} async-done(((bf16[8,32,64]{1,0,2:T(8,128)(2,1)}), bf16[8,32,4096]{1,0,2:T(8,128)(2,1)}) %all-gather.6.cloned.1.call-update) | async-done | bytes 2097168 | tf_op jit(solution)/shard_map/all_gather | solution.py:42
  204.1 9.4 %copy.48 = bf16[8,32,4096]{2,1,0:T(8,128)(2,1)} copy(bf16[8,32,4096]{1,0,2:T(8,128)(2,1)} %all-gather.6.cloned.1.call-done) | data formatting | bytes 4194304 | tf_op jit(solution)/shard_map/all_gather | solution.py:42
  213.5 2.5 fusion.2
  216.3 0.8 fusion.12
  217.1 70.8 %all-gather.8.cloned.1.call-done = bf16[4096,256]{1,0:T(8,128)(2,1)} async-done(((bf16[64,256]{1,0:T(8,128)(2,1)}), bf16[4096,256]{1,0:T(8,128)(2,1)}) %all-gather.8.cloned.1.call-update) | async-done | bytes 2097168 | tf_op jit(solution)/shard_map/all_gather | solution.py:74
  287.8 3.1 fusion.15
  291.0 1.3 fusion.34
  292.6 2.9 fusion
  295.5 0.9 copy-done.2
  296.6 181.5 %all-reduce.3.cloned.1.call-done = f32[256,256]{0,1:T(8,128)} async-done(((f32[256,256]{0,1:T(8,128)}), f32[256,256]{0,1:T(8,128)}) %all-reduce.3.cloned.1.call-update) | async-done | bytes 262160 | tf_op jit(solution)/shard_map/psum | solution.py:83
  478.1 1.0 convert_add_fusion
  479.3 11.7 %cholesky.50 = f32[128,128]{1,0:T(8,128)S(1)} custom-call(f32[128,128]{1,0:T(8,128)S(1)} %cholesky.118), custom_call_target="Cholesky" | custom-call | tf_op jit(solution)/shard_map/jit(cholesky)/cholesky | solution.py:85
  491.0 9.8 %custom-call.18 = f32[1,128,128]{1,2,0:T(8,128)S(1)} custom-call(f32[1,128,128]{2,1,0:T(8,128)S(1)} %get-tuple-element.42), custom_call_target="InvertDiagBlocksLowerTriangular" | custom-call | tf_op jit(solution)/shard_map/jit(cholesky)/cholesky | solution.py:85
  501.3 11.7 %cholesky.105 = f32[128,128]{1,0:T(8,128)S(1)} custom-call(f32[128,128]{1,0:T(8,128)S(1)} %convolution_subtract_fusion.2), custom_call_target="Cholesky" | custom-call | tf_op jit(solution)/shard_map/jit(cholesky)/cholesky | solution.py:85
  515.1 4.2 while.1
  515.9 1.4 bitcast_dynamic-update-slice_fusion.2
  517.9 1.4 bitcast_dynamic-update-slice_fusion.2
  519.3 19.7 %custom-call.19 = f32[2,128,128]{1,2,0:T(8,128)S(1)} custom-call(f32[2,128,128]{2,1,0:T(8,128)S(1)} %get-tuple-element.10), custom_call_target="InvertDiagBlocksLowerTriangular" | custom-call | tf_op jit(solution)/shard_map/jit(_cho_solve)/triangular_solve | solution.py:86
  540.6 93.1 %reduce-scatter.2.cloned.1.call-done = f32[256,64]{0,1:T(8,128)} async-done(((f32[256,4096]{0,1:T(8,128)}), f32[256,64]{0,1:T(8,128)}) %reduce-scatter.2.cloned.1.call-update) | async-done | bytes 65552 | tf_op jit(solution)/shard_map/reduce_scatter | solution.py:58
  633.7 0.8 convert_element_type.37
  635.4 6.7 %all-to-all-start.2 = ((bf16[8,2,1024]{2,1,0:T(2,128)(2,1)}), bf16[8,2,1024]{2,1,0:T(2,128)(2,1)S(1)}, u32[]{:S(2)}, u32[]{:S(2)}) async-start(bf16[8,2,1024]{2,1,0:T(2,128)(2,1)} %reshape.117), calls=%async_computation.3 | async-start | bytes 65536 | tf_op jit(solution)/shard_map/all_to_all | solution.py:61
  642.8 0.8 copy.53
  643.7 6.5 all-to-all-done.2
  (63 shorter events, 10.8 us)
Async XLA Ops:
  7.2 206.4 %copy-start = (bf16[1,224,4096]{2,1,0:T(8,128)(2,1)S(1)}, bf16[1,224,4096]{2,1,0:T(8,128)(2,1)}, u32[]{:S(2)}) copy-start(bf16[1,224,4096]{2,1,0:T(8,128)(2,1)} %param.12) | copy-start | bytes 5505028
  7.2 107.5 %all-gather.4.cloned.1.call-start = ((), (), s32[]{:S(2)}) async-start(), calls=%async_computation.4 | async-start | bytes 8519680 | tf_op jit(solution)/shard_map/all_gather | solution.py:43
  27.1 177.0 %all-gather.6.cloned.1.call-start = ((), (), s32[]{:S(2)}) async-start(), calls=%async_computation.5 | async-start | bytes 8519680 | tf_op jit(solution)/shard_map/all_gather | solution.py:42
  39.7 248.2 %all-gather.8.cloned.1.call-start = ((), (), s32[]{:S(2)}) async-start(), calls=%async_computation.7 | async-start | bytes 2129920 | tf_op jit(solution)/shard_map/all_gather | solution.py:74
  40.4 437.7 %all-reduce.3.cloned.1.call-start = ((), (), s32[]{:S(2)}) async-start(), calls=%async_computation.8 | async-start | bytes 524288 | tf_op jit(solution)/shard_map/psum | solution.py:83
  213.5 2.6 copy-start.1
  213.5 2.8 copy-start.3
  292.4 341.3 %reduce-scatter.2.cloned.1.call-start = ((), (), s32[]{:S(2)}) async-start(), calls=%async_computation.6 | async-start | bytes 4259840 | tf_op jit(solution)/shard_map/reduce_scatter | solution.py:58
  295.5 0.9 copy-start.2
  635.4 14.8 %all-to-all-start.2 = ((bf16[8,2,1024]{2,1,0:T(2,128)(2,1)}), bf16[8,2,1024]{2,1,0:T(2,128)(2,1)S(1)}, u32[]{:S(2)}, u32[]{:S(2)}) async-start(bf16[8,2,1024]{2,1,0:T(2,128)(2,1)} %reshape.117), calls=%async_computation.3 | async-start | bytes 65536 | tf_op jit(solution)/shard_map/all_to_all | solution.py:61
Sparse Core Ops, SparseCore 0:
  27.3 87.3 all-gather.3
  118.6 85.4 all-gather.5
  207.5 80.3 all-gather.7
  292.5 185.5 all-reduce.2
  482.6 151.0 reduce-scatter.1
where the time goes:
time: 658 us
  waiting for transfers between devices  507 us (77%)
  other arithmetic  58.9 us (9%)
  local copies, waits for them, and re-layouts  28.5 us (4%)
  blocking collectives  25.3 us (4%)
  matrix products  15.3 us (2%)
  between operations  15.3 us (2%)
  starting transfers between devices  7.12 us (1%)
    psum x1, waiting for transfers between devices, per_device(): gram_total = lax.psum(gram_part, 'dp') / total_hidden  181 us
    reduce_scatter x1, waiting for transfers between devices, per_device(): lax.psum_scatter(partial_value, 'dp', scatter_dimension=1, tiled=True)  93.1 us
    all_gather x1, waiting for transfers between devices, per_device(): lax.all_gather(x_recv, 'dp', axis=2, tiled=True)  80.1 us
    all_gather x1, waiting for transfers between devices, per_device(): lax.all_gather(dy_recv, 'dp', axis=2, tiled=True)  74.2 us
    all_gather x1, waiting for transfers between devices, per_device(): basis_full = lax.all_gather(basis, 'dp', axis=0, tiled=True)  70.8 us
    another operation x6, other arithmetic, per_device(): jnp.linalg.cholesky(merged + damping * jnp.eye(merged.shape[0], dtype=jnp...  34 us
    another operation x3, other arithmetic, per_device(): solved = damping * jax.scipy.linalg.cho_solve((factor, True), coefficients)  19.7 us
    all_to_all x1, blocking collectives, per_device(): lax.all_to_all(dy_send, 'expert', split_axis=0, concat_axis=0, tiled=True)  14.9 us
  transfers between devices with their start and end apart: 6, of which 6 were waited for; matrix products, arithmetic and copies ran while one was open for 14% of the time, Pallas kernels for 0%

commit v1 on v0

--- a/solution.py
+++ b/solution.py
@@ -6,6 +6,11 @@
 decay_rate = 0.9
 damping = 1.0
 highest = lax.Precision.HIGHEST
+
+
+def gather_and_add(array, axis):
+    shards = lax.all_gather(array, axis)
+    return jnp.sum(shards, axis=0)
 
 
 def per_device(tokens, cotangent, gate_logit, routes, w_up, w_down, basis, sketch):
@@ -80,7 +85,7 @@
     )
     gram_part = jnp.dot(coefficients, coefficients.T, precision=highest)
     total_hidden = w_up.shape[1] * lax.axis_size("dp")
-    gram_total = lax.psum(gram_part, "dp") / total_hidden
+    gram_total = gather_and_add(gram_part, "dp") / total_hidden
     merged = decay_rate * sketch[0] + gram_total
     factor = jnp.linalg.cholesky(merged + damping * jnp.eye(merged.shape[0], dtype=jnp.float32))
     solved = damping * jax.scipy.linalg.cho_solve((factor, True), coefficients)

time: 658 us -> 630 us (0.957)
  the two profiles are of different devices: /device:TPU:2 before, /device:TPU:1 now
where the time goes in v1:
time: 630 us; the launch traced here: 629 us
  waiting for transfers between devices  475 us (75%)
  other arithmetic  65.1 us (10%)
  local copies, waits for them, and re-layouts  27.9 us (4%)
  blocking collectives  23.6 us (4%)
  between operations  15.4 us (2%)
  matrix products  15.3 us (2%)
  starting transfers between devices  6.66 us (1%)
    reduce_scatter x1, waiting for transfers between devices, per_device(): lax.psum_scatter(partial_value, 'dp', scatter_dimension=1, tiled=True)  145 us
    all_gather x1, waiting for transfers between devices, gather_and_add(): shards = lax.all_gather(array, axis)  96.9 us
    all_gather x1, waiting for transfers between devices, per_device(): lax.all_gather(x_recv, 'dp', axis=2, tiled=True)  80 us
    all_gather x1, waiting for transfers between devices, per_device(): lax.all_gather(dy_recv, 'dp', axis=2, tiled=True)  78.5 us
    all_gather x1, waiting for transfers between devices, per_device(): basis_full = lax.all_gather(basis, 'dp', axis=0, tiled=True)  67.5 us
    another operation x6, other arithmetic, per_device(): jnp.linalg.cholesky(merged + damping * jnp.eye(merged.shape[0], dtype=jnp...  34 us
    another operation x3, other arithmetic, per_device(): solved = damping * jax.scipy.linalg.cho_solve((factor, True), coefficients)  19.9 us
    all_to_all x1, blocking collectives, per_device(): lax.all_to_all(dy_send, 'expert', split_axis=0, concat_axis=0, tiled=True)  14.3 us
  transfers between devices with their start and end apart: 6, of which 6 were waited for; matrix products, arithmetic and copies ran while one was open for 5% of the time, Pallas kernels for 0%

profile of v1, /device:TPU:1, one launch (start us, length us, event | category | flops | bytes accessed | tf_op | source)
XLA Modules:
  0.0 629.0 jit_solution(15920578633638807088)
XLA Ops:
  7.2 0.8 convert_reduce_fusion.1
  10.1 0.9 fusion.16
  11.3 14.3 %all_to_all.15 = bf16[8,2,1024]{2,1,0:T(2,128)(2,1)S(1)} all-to-all(bf16[8,2,1024]{2,1,0:T(2,128)(2,1)S(1)} %reshape.123), channel_id=1, replica_groups=mesh['dp'=64,'expert'=8] {'expert'}, dimensions={0} | all-to-all | bytes 65536 | tf_op jit(solution)/shard_map/all_to_all | solution.py:44
  25.7 0.8 copy.42
  26.6 0.9 convolution_convert_fusion.1
  27.7 9.2 %all_to_all.16 = bf16[8,2,1024]{2,1,0:T(2,128)(2,1)S(1)} all-to-all(bf16[8,2,1024]{2,1,0:T(2,128)(2,1)S(1)} %reshape.125), channel_id=1, replica_groups=mesh['dp'=64,'expert'=8] {'expert'}, dimensions={0} | all-to-all | bytes 65536 | tf_op jit(solution)/shard_map/all_to_all | solution.py:43
  37.1 0.8 copy.45
  38.7 78.5 %all-gather.6.cloned.1.call-done = bf16[8,32,4096]{1,0,2:T(8,128)(2,1)} async-done(((bf16[8,32,64]{1,0,2:T(8,128)(2,1)}), bf16[8,32,4096]{1,0,2:T(8,128)(2,1)}) %all-gather.6.cloned.1.call-update) | async-done | bytes 2097168 | tf_op jit(solution)/shard_map/all_gather | solution.py:48
  117.2 9.4 %copy.43 = bf16[8,32,4096]{2,1,0:T(8,128)(2,1)} copy(bf16[8,32,4096]{1,0,2:T(8,128)(2,1)} %all-gather.6.cloned.1.call-done) | data formatting | bytes 4194304 | tf_op jit(solution)/shard_map/all_gather | solution.py:48
  126.5 80.0 %all-gather.8.cloned.1.call-done = bf16[8,32,4096]{1,0,2:T(8,128)(2,1)} async-done(((bf16[8,32,64]{1,0,2:T(8,128)(2,1)}), bf16[8,32,4096]{1,0,2:T(8,128)(2,1)}) %all-gather.8.cloned.1.call-update) | async-done | bytes 2097168 | tf_op jit(solution)/shard_map/all_gather | solution.py:47
  206.6 9.4 %copy.46 = bf16[8,32,4096]{2,1,0:T(8,128)(2,1)} copy(bf16[8,32,4096]{1,0,2:T(8,128)(2,1)} %all-gather.8.cloned.1.call-done) | data formatting | bytes 4194304 | tf_op jit(solution)/shard_map/all_gather | solution.py:47
  216.0 2.5 fusion.2
  218.7 0.8 fusion.12
  219.5 2.9 fusion
  222.5 67.5 %all-gather.10.cloned.1.call-done = bf16[4096,256]{1,0:T(8,128)(2,1)} async-done(((bf16[64,256]{1,0:T(8,128)(2,1)}), bf16[4096,256]{1,0:T(8,128)(2,1)}) %all-gather.10.cloned.1.call-update) | async-done | bytes 2097168 | tf_op jit(solution)/shard_map/all_gather | solution.py:79
  290.0 3.1 fusion.15
  293.2 1.3 fusion.34
  294.7 144.6 %reduce-scatter.2.cloned.1.call-done = f32[256,64]{0,1:T(8,128)} async-done(((f32[256,4096]{0,1:T(8,128)}), f32[256,64]{0,1:T(8,128)}) %reduce-scatter.2.cloned.1.call-update) | async-done | bytes 65552 | tf_op jit(solution)/shard_map/reduce_scatter | solution.py:63
  439.3 0.8 convert_element_type.37
  441.0 6.5 %all-to-all-start.2 = ((bf16[8,2,1024]{2,1,0:T(2,128)(2,1)}), bf16[8,2,1024]{2,1,0:T(2,128)(2,1)S(1)}, u32[]{:S(2)}, u32[]{:S(2)}) async-start(bf16[8,2,1024]{2,1,0:T(2,128)(2,1)} %reshape.127), calls=%async_computation.3 | async-start | bytes 65536 | tf_op jit(solution)/shard_map/all_to_all | solution.py:66
  447.4 6.9 %all-to-all-done.2 = bf16[8,2,1024]{2,1,0:T(2,128)(2,1)S(1)} async-done(((bf16[8,2,1024]{2,1,0:T(2,128)(2,1)}), bf16[8,2,1024]{2,1,0:T(2,128)(2,1)S(1)}, u32[]{:S(2)}, u32[]{:S(2)}) %all-to-all-start.2) | async-done | bytes 32800 | tf_op jit(solution)/shard_map/all_to_all | solution.py:66
  454.4 0.7 convolution_convert_fusion.2
  455.2 96.9 %all-gather.12.cloned.1.call-done = f32[16384,256]{1,0:T(8,128)} async-done(((f32[256,256]{1,0:T(8,128)}), f32[16384,256]{1,0:T(8,128)}) %all-gather.12.cloned.1.call-update) | async-done | bytes 16777232 | tf_op jit(solution)/shard_map/all_gather | solution.py:12
  552.1 6.8 %reduce_sum.49 = f32[256,256]{1,0:T(8,128)S(1)} reduce(f32[64,256,256]{2,1,0:T(8,128)} %bitcast.84, f32[]{:T(128)} %constant.99.clone.1), dimensions={0}, to_apply=%region_6.7 | reduce | flops 4128768 | bytes 17039364 | tf_op jit(solution)/shard_map/reduce_sum | solution.py:13
  559.3 11.7 %cholesky.50 = f32[128,128]{1,0:T(8,128)S(1)} custom-call(f32[128,128]{1,0:T(8,128)S(1)} %cholesky.118), custom_call_target="Cholesky" | custom-call | tf_op jit(solution)/shard_map/jit(cholesky)/cholesky | solution.py:90
  571.1 0.8 copy.51
  572.0 9.8 %custom-call.18 = f32[1,128,128]{1,2,0:T(8,128)S(1)} custom-call(f32[1,128,128]{2,1,0:T(8,128)S(1)} %get-tuple-element.40), custom_call_target="InvertDiagBlocksLowerTriangular" | custom-call | tf_op jit(solution)/shard_map/jit(cholesky)/cholesky | solution.py:90
  582.2 11.7 %cholesky.105 = f32[128,128]{1,0:T(8,128)S(1)} custom-call(f32[128,128]{1,0:T(8,128)S(1)} %convolution_subtract_fusion.2), custom_call_target="Cholesky" | custom-call | tf_op jit(solution)/shard_map/jit(cholesky)/cholesky | solution.py:90
  596.2 4.1 while.1
  596.8 1.4 bitcast_dynamic-update-slice_fusion.2
  598.8 1.4 bitcast_dynamic-update-slice_fusion.2
  600.3 19.9 %custom-call.19 = f32[2,128,128]{1,2,0:T(8,128)S(1)} custom-call(f32[2,128,128]{2,1,0:T(8,128)S(1)} %get-tuple-element.10), custom_call_target="InvertDiagBlocksLowerTriangular" | custom-call | tf_op jit(solution)/shard_map/jit(_cho_solve)/triangular_solve | solution.py:91
  (66 shorter events, 10.3 us)
Async XLA Ops:
  7.2 208.8 %copy-start = (bf16[1,224,4096]{2,1,0:T(8,128)(2,1)S(1)}, bf16[1,224,4096]{2,1,0:T(8,128)(2,1)}, u32[]{:S(2)}) copy-start(bf16[1,224,4096]{2,1,0:T(8,128)(2,1)} %param.12) | copy-start | bytes 5505028
  7.2 110.0 %all-gather.6.cloned.1.call-start = ((), (), s32[]{:S(2)}) async-start(), calls=%async_computation.4 | async-start | bytes 8519680 | tf_op jit(solution)/shard_map/all_gather | solution.py:48
  26.5 180.0 %all-gather.8.cloned.1.call-start = ((), (), s32[]{:S(2)}) async-start(), calls=%async_computation.5 | async-start | bytes 8519680 | tf_op jit(solution)/shard_map/all_gather | solution.py:47
  37.9 252.1 %all-gather.10.cloned.1.call-start = ((), (), s32[]{:S(2)}) async-start(), calls=%async_computation.7 | async-start | bytes 2129920 | tf_op jit(solution)/shard_map/all_gather | solution.py:79
  38.6 400.6 %reduce-scatter.2.cloned.1.call-start = ((), (), s32[]{:S(2)}) async-start(), calls=%async_computation.6 | async-start | bytes 4259840 | tf_op jit(solution)/shard_map/reduce_scatter | solution.py:63
  216.0 2.5 copy-start.1
  216.0 2.8 copy-start.3
  222.4 72.1 %copy-start.2 = (f32[1,256,256]{2,1,0:T(8,128)S(1)}, f32[1,256,256]{2,1,0:T(8,128)}, u32[]{:S(2)}) copy-start(f32[1,256,256]{2,1,0:T(8,128)} %param.15) | copy-start | bytes 786436
  222.4 329.6 %all-gather.12.cloned.1.call-start = ((), (), s32[]{:S(2)}) async-start(), calls=%async_computation.8 | async-start | bytes 17039360 | tf_op jit(solution)/shard_map/all_gather | solution.py:12
  441.0 13.3 %all-to-all-start.2 = ((bf16[8,2,1024]{2,1,0:T(2,128)(2,1)}), bf16[8,2,1024]{2,1,0:T(2,128)(2,1)S(1)}, u32[]{:S(2)}, u32[]{:S(2)}) async-start(bf16[8,2,1024]{2,1,0:T(2,128)(2,1)} %reshape.127), calls=%async_computation.3 | async-start | bytes 65536 | tf_op jit(solution)/shard_map/all_to_all | solution.py:66
Sparse Core Ops, SparseCore 0:
  26.7 90.4 all-gather.5
  121.1 85.4 all-gather.7
  209.9 80.0 all-gather.9
  294.6 144.6 reduce-scatter.1
  443.0 108.9 all-gather.11
